TPU v7x, 32 devices: a whole 2x2x4 slice. The times are simulated.
32 devices in a mesh: seq: 8 (over z, y), head: 4 (over x, core).
Axes of the slice: x: 2, y: 2, z: 4, core: 2. Of those that a mesh axis runs over, the one named last changes fastest.
Arguments:
- queries: bfloat16 [1024, 4096], P(('seq', 'head')), may hold values from -6 to 6
- keys: bfloat16 [1024, 4096], P(('seq', 'head')), may hold values from -0.5 to 0.5
- values: bfloat16 [1024, 4096], P(('seq', 'head')), may hold values from -6 to 6
- log_decay: float32 [1024, 32], P('seq', 'head'), may hold values from -2 to 0, as said below
- out_grad: bfloat16 [1024, 4096], P('seq', 'head'), may hold values from -6 to 6
Outputs:
- attn_out: bfloat16 [1024, 4096], P('seq', 'head')
- query_grad: bfloat16 [1024, 4096], P('seq', 'head')
- key_grad: bfloat16 [1024, 4096], P('seq', 'head')
- value_grad: bfloat16 [1024, 4096], P('seq', 'head')
Inputs may be any that keep to these rules, and one draw needn't show every extreme that they name: `log_decay`: never positive.
All inputs are finite; a program needn't handle non-finite values.
Results may differ from a plain program's by a relative error of at most 0.0056.
Values may be sent and summed in bfloat16 or wider, within the bound.
No kernel may reach another device: no remote copies, remote signals or barrier semaphores. Data moves between devices by JAX's collectives and lax.ppermute only.
A program may use at most 64 MiB of HBM per device.

v0:
```python
import jax
import jax.numpy as jnp
from jax import lax
from jax.sharding import PartitionSpec as P

DK = 128
split_mode = lax.Precision.HIGH


def prefix(array, axis, combine, identity, reverse):
    length, index = (lax.axis_size(axis), lax.axis_index(axis))
    everything = jax.tree.map(lambda part: lax.all_gather(part, axis), array)
    start = jax.tree.map(
        lambda part, zero: jnp.broadcast_to(jnp.asarray(zero, part.dtype), part.shape),
        array,
        identity,
    )

    def lap(k, before):
        at = length - 1 - k if reverse else k
        reached = at > index if reverse else at < index
        new = combine(before, jax.tree.map(lambda part: part[at], everything))
        return jax.tree.map(lambda a, b: jnp.where(reached, a, b), new, before)

    return lax.fori_loop(0, length, lap, start)


def decay_table(running):
    block_rows = running.shape[0]
    gaps = running.T[:, :, None] - running.T[:, None, :]
    causal = lax.broadcasted_iota(jnp.int32, (block_rows, block_rows), 0) >= lax.broadcasted_iota(
        jnp.int32, (block_rows, block_rows), 1
    )
    return jnp.where(causal[None], jnp.exp(jnp.where(causal[None], gaps, 0.0)), 0.0)


def chained(earlier, later):
    return (earlier[0] * later[0], later[0][:, None, None] * earlier[1] + later[1])


def pass_states(factor, own_state):
    identity = (jnp.ones_like(factor), jnp.zeros_like(own_state))
    return prefix((factor, own_state), "seq", chained, identity, False)[1]


def pass_gradients(factor, own_grad):
    identity = (jnp.ones_like(factor), jnp.zeros_like(own_grad))
    return prefix((factor, own_grad), "seq", chained, identity, True)[1]


def local(queries, keys, values, log_decay, out_grad):
    block_rows = log_decay.shape[0]
    head_count = log_decay.shape[1]
    layout = (block_rows, head_count, DK)
    running = jnp.cumsum(log_decay, axis=0)
    final = running[-1]
    factor = jnp.exp(final)
    rising = jnp.exp(running)[:, :, None]
    tail_weight = jnp.exp(final[None, :] - running)[:, :, None]
    query_all, key_all, value_all = (
        lax.all_to_all(queries, "head", split_axis=1, concat_axis=0, tiled=True),
        lax.all_to_all(keys, "head", split_axis=1, concat_axis=0, tiled=True),
        lax.all_to_all(values, "head", split_axis=1, concat_axis=0, tiled=True),
    )
    key_rows = key_all.reshape(layout)
    value_rows = value_all.reshape(layout)
    key_wide = key_rows.astype(jnp.float32)
    state_in = pass_states(
        factor,
        jnp.einsum(
            "thd,the->hde",
            key_wide * tail_weight,
            value_rows.astype(jnp.float32),
            precision=split_mode,
        ),
    )
    query_rows = query_all.reshape(layout)
    table = decay_table(running)
    query_wide = query_rows.astype(jnp.float32)
    scores = jnp.einsum("thd,shd->hts", query_rows, key_rows, preferred_element_type=jnp.float32)
    weighted = (scores * table).astype(jnp.bfloat16)
    inner = jnp.einsum("hts,she->the", weighted, value_rows, preferred_element_type=jnp.float32)
    mixed = inner + rising * jnp.einsum("thd,hde->the", query_wide, state_in, precision=split_mode)
    inverse = lax.rsqrt(jnp.mean(mixed * mixed, axis=-1) + 1e-06)[:, :, None]
    normed = mixed * inverse
    grad_wide = out_grad.reshape(layout).astype(jnp.float32)
    out_delta = (
        inverse * (grad_wide - normed * jnp.mean(grad_wide * normed, axis=-1, keepdims=True))
    ).astype(jnp.bfloat16)
    delta_wide = out_delta.astype(jnp.float32)
    own_grad = jnp.einsum("thd,the->hde", query_wide * rising, delta_wide, precision=split_mode)
    grad_state = pass_gradients(factor, own_grad)
    delta_scores = jnp.einsum(
        "the,she->hts", out_delta, value_rows, preferred_element_type=jnp.float32
    )
    delta_weighted = (delta_scores * table).astype(jnp.bfloat16)
    query_grad = jnp.einsum(
        "hts,shd->thd", delta_weighted, key_rows, preferred_element_type=jnp.float32
    )
    query_grad = query_grad + rising * jnp.einsum(
        "the,hde->thd", delta_wide, state_in, precision=split_mode
    )
    key_grad = jnp.einsum(
        "hts,thd->shd", delta_weighted, query_rows, preferred_element_type=jnp.float32
    )
    key_grad = key_grad + tail_weight * jnp.einsum(
        "she,hde->shd", value_rows.astype(jnp.float32), grad_state, precision=split_mode
    )
    value_grad = jnp.einsum("hts,the->she", weighted, out_delta, preferred_element_type=jnp.float32)
    value_grad = value_grad + tail_weight * jnp.einsum(
        "shd,hde->she", key_rows.astype(jnp.float32), grad_state, precision=split_mode
    )
    flat = (block_rows, head_count * DK)
    return (
        normed.astype(jnp.bfloat16).reshape(flat),
        query_grad.astype(jnp.bfloat16).reshape(flat),
        key_grad.astype(jnp.bfloat16).reshape(flat),
        value_grad.astype(jnp.bfloat16).reshape(flat),
    )


def solution(mesh):
    placed = (
        P(("seq", "head"), None),
        P(("seq", "head"), None),
        P(("seq", "head"), None),
        P("seq", "head"),
        P("seq", "head"),
    )
    return jax.shard_map(
        local,
        mesh=mesh,
        in_specs=placed,
        out_specs=(P("seq", "head"), P("seq", "head"), P("seq", "head"), P("seq", "head")),
        check_vma=False,
    )
```

profile of v0, /device:TPU:0, one launch (start us, length us, event | category | flops | bytes accessed | tf_op | source)
XLA Modules:
  0.0 206.9 jit_solution(703860958930601982)
XLA Ops:
  7.2 1.7 copy.122
  8.9 4.2 %all-to-all-start.1 = ((bf16[32,4,1024]{2,0,1:T(8,128)(2,1)}), bf16[32,4,1024]{2,0,1:T(8,128)(2,1)S(1)}, u32[]{:S(2)}, u32[]{:S(2)}) async-start(bf16[32,4,1024]{2,0,1:T(8,128)(2,1)} %bitcast.104), calls=%async_computation.1 | async-start | bytes 524288 | tf_op jit(solution)/shard_map/all_to_all | solution.py:62
  13.9 1.7 copy.121
  15.8 3.4 %all-to-all-done.1 = bf16[32,4,1024]{2,0,1:T(8,128)(2,1)S(1)} async-done(((bf16[32,4,1024]{2,0,1:T(8,128)(2,1)}), bf16[32,4,1024]{2,0,1:T(8,128)(2,1)S(1)}, u32[]{:S(2)}, u32[]{:S(2)}) %all-to-all-start.1) | async-done | bytes 262176 | tf_op jit(solution)/shard_map/all_to_all | solution.py:62
  19.2 3.4 %all-to-all-start.2 = ((bf16[32,4,1024]{2,0,1:T(8,128)(2,1)}), bf16[32,4,1024]{2,0,1:T(8,128)(2,1)S(1)}, u32[]{:S(2)}, u32[]{:S(2)}) async-start(bf16[32,4,1024]{2,0,1:T(8,128)(2,1)} %bitcast.103), calls=%async_computation.2 | async-start | bytes 524288 | tf_op jit(solution)/shard_map/all_to_all | solution.py:63
  23.0 5.5 %all-to-all-done.2 = bf16[32,4,1024]{2,0,1:T(8,128)(2,1)S(1)} async-done(((bf16[32,4,1024]{2,0,1:T(8,128)(2,1)}), bf16[32,4,1024]{2,0,1:T(8,128)(2,1)S(1)}, u32[]{:S(2)}, u32[]{:S(2)}) %all-to-all-start.2) | async-done | bytes 262176 | tf_op jit(solution)/shard_map/all_to_all | solution.py:63
  30.4 3.4 %all-to-all-start = ((bf16[32,4,1024]{2,0,1:T(8,128)(2,1)}), bf16[32,4,1024]{2,0,1:T(8,128)(2,1)S(1)}, u32[]{:S(2)}, u32[]{:S(2)}) async-start(bf16[32,4,1024]{2,0,1:T(8,128)(2,1)} %bitcast.105), calls=%async_computation | async-start | bytes 524288 | tf_op jit(solution)/shard_map/all_to_all | solution.py:61
  34.2 21.9 %all-gather.2 = f32[8,1,8]{2,1,0:T(1,128)S(1)} all-gather(f32[1,1,8]{2,1,0:T(1,128)S(1)} %get-tuple-element.301), channel_id=1, replica_groups=mesh['seq'=8,'head'=4] {'seq'}, dimensions={0}, use_global_device_ids=true | all-gather | bytes 288 | tf_op jit(solution)/shard_map/all_gather | solution.py:12
  56.8 46.8 %all-gather.6.cloned.1.call-done = f32[64,128,128]{2,1,0:T(8,128)} async-done(((f32[8,128,128]{2,1,0:T(8,128)}), f32[64,128,128]{2,1,0:T(8,128)}) %all-gather.6.cloned.1.call-update) | async-done | bytes 4194320 | tf_op jit(solution)/shard_map/all_gather | solution.py:12
  103.6 9.7 %while.30 = (s32[]{:T(128)}, f32[8,128,128]{2,1,0:T(8,128)S(1)}, s32[]{:T(128)}, f32[8,8]{1,0:T(8,128)S(1)}, f32[8,8,128,128]{3,2,1,0:T(8,128)}, /*index=5*/s32[]{:T(128)}, s32[]{:T(128)}) while((s32[]{:T(128)}, f32[8,128,128]{2,1,0:T(8,128)S(1)}, s32[]{:T(128)}, f32[8,8]{1,0:T(8,128)S(1)}, f32[8,8,128,128]{3,2,1,0:T(8,128)}, ...), condition=%wide.region_2.3_spmd.clone, body=%wide.region_1.2_spmd.clone.sunk | while | flops 524292 | bytes 1573073 | solution.py:25
  104.8 1.2 fusion.51
  108.5 1.2 fusion.51
  109.7 1.2 fusion.51
  110.9 1.2 fusion.51
  114.4 1.3 fusion.18
  118.3 68.8 %all-gather.8.cloned.1.call-done = f32[64,128,128]{2,1,0:T(8,128)} async-done(((f32[8,128,128]{2,1,0:T(8,128)}), f32[64,128,128]{2,1,0:T(8,128)}) %all-gather.8.cloned.1.call-update) | async-done | bytes 4194320 | tf_op jit(solution)/shard_map/all_gather | solution.py:12
  187.2 9.8 %while.31 = (s32[]{:T(128)}, f32[8,128,128]{2,1,0:T(8,128)S(1)}, s32[]{:T(128)}, f32[8,8]{1,0:T(8,128)S(1)}, f32[8,8,128,128]{3,2,1,0:T(8,128)}, /*index=5*/s32[]{:T(128)}, s32[]{:T(128)}, s32[]{:T(128)}, s32[]{:T(128)}) while((s32[]{:T(128)}, f32[8,128,128]{2,1,0:T(8,128)S(1)}, s32[]{:T(128)}, f32[8,8]{1,0:T(8,128)S(1)}, ...), condition=%wide.region_6.7_spmd.clone, body=%wide.region_5.6_spmd.clone.sunk | while | flops 524296 | bytes 1573135 | solution.py:25
  188.4 1.2 fusion.52
  189.6 1.2 fusion.52
  190.8 1.2 fusion.52
  192.1 1.2 fusion.52
  193.3 1.2 fusion.52
  194.5 1.2 fusion.52
  195.7 1.2 fusion.52
  (66 shorter events, 16.9 us)
Async XLA Ops:
  7.2 22.5 %copy-start = (bf16[32,4096]{1,0:T(8,128)(2,1)S(1)}, bf16[32,4096]{1,0:T(8,128)(2,1)}, u32[]{:S(2)}) copy-start(bf16[32,4096]{1,0:T(8,128)(2,1)} %param.9) | copy-start | bytes 786436
  7.2 26.9 %copy-start.1 = (bf16[128,1024]{1,0:T(8,128)(2,1)S(1)}, bf16[128,1024]{1,0:T(8,128)(2,1)}, u32[]{:S(2)}) copy-start(bf16[128,1024]{1,0:T(8,128)(2,1)} %param.13) | copy-start | bytes 786436
  8.9 10.2 %all-to-all-start.1 = ((bf16[32,4,1024]{2,0,1:T(8,128)(2,1)}), bf16[32,4,1024]{2,0,1:T(8,128)(2,1)S(1)}, u32[]{:S(2)}, u32[]{:S(2)}) async-start(bf16[32,4,1024]{2,0,1:T(8,128)(2,1)} %bitcast.104), calls=%async_computation.1 | async-start | bytes 524288 | tf_op jit(solution)/shard_map/all_to_all | solution.py:62
  19.2 9.4 %all-to-all-start.2 = ((bf16[32,4,1024]{2,0,1:T(8,128)(2,1)}), bf16[32,4,1024]{2,0,1:T(8,128)(2,1)S(1)}, u32[]{:S(2)}, u32[]{:S(2)}) async-start(bf16[32,4,1024]{2,0,1:T(8,128)(2,1)} %bitcast.103), calls=%async_computation.2 | async-start | bytes 524288 | tf_op jit(solution)/shard_map/all_to_all | solution.py:63
  22.6 81.1 %all-gather.6.cloned.1.call-start = ((), (), s32[]{:S(2)}) async-start(), calls=%async_computation.3 | async-start | bytes 4718592 | tf_op jit(solution)/shard_map/all_gather | solution.py:12
  30.4 25.7 %all-to-all-start = ((bf16[32,4,1024]{2,0,1:T(8,128)(2,1)}), bf16[32,4,1024]{2,0,1:T(8,128)(2,1)S(1)}, u32[]{:S(2)}, u32[]{:S(2)}) async-start(bf16[32,4,1024]{2,0,1:T(8,128)(2,1)} %bitcast.105), calls=%async_computation | async-start | bytes 524288 | tf_op jit(solution)/shard_map/all_to_all | solution.py:61
  33.9 153.3 %all-gather.8.cloned.1.call-start = ((), (), s32[]{:S(2)}) async-start(), calls=%async_computation.4 | async-start | bytes 4718592 | tf_op jit(solution)/shard_map/all_gather | solution.py:12
Sparse Core Ops, SparseCore 0:
  29.8 73.7 all-gather.5
  115.8 71.3 all-gather.7
where the time goes:
time: 208 us; the launch traced here: 207 us
  waiting for transfers between devices  125 us (60%)
  blocking collectives  21.9 us (11%)
  other arithmetic  19.2 us (9%)
  between operations  14.3 us (7%)
  starting transfers between devices  11.1 us (5%)
  local copies, waits for them, and re-layouts  9.4 us (5%)
  matrix products  5.79 us (3%)
    all_gather x2, waiting for transfers between devices, prefix(): everything = jax.tree.map(lambda part: lax.all_gather(part, axis), array)  116 us
    all_gather x1, blocking collectives, prefix(): everything = jax.tree.map(lambda part: lax.all_gather(part, axis), array)  21.9 us
    select_n x16, other arithmetic, lap(): return jax.tree.map(lambda a, b: jnp.where(reached, a, b), new, before)  18.8 us
    all_to_all x1, waiting for transfers between devices, local(): lax.all_to_all(values, 'head', split_axis=1, concat_axis=0, tiled=True)  5.53 us
    unnamed x13, local copies, waits for them, and re-layouts  4.54 us
    all_to_all x1, starting transfers between devices, local(): lax.all_to_all(keys, 'head', split_axis=1, concat_axis=0, tiled=True)  4.24 us
  transfers between devices with their start and end apart: 5, of which 4 were waited for; matrix products, arithmetic and copies ran while one was open for 4% of the time, Pallas kernels for 0%

commit v1 on v0

--- a/solution.py
+++ b/solution.py
@@ -60,7 +60,12 @@
     query_all, key_all, value_all = (
         lax.all_to_all(queries, "head", split_axis=1, concat_axis=0, tiled=True),
         lax.all_to_all(keys, "head", split_axis=1, concat_axis=0, tiled=True),
-        lax.all_to_all(values, "head", split_axis=1, concat_axis=0, tiled=True),
+        jnp.concatenate(
+            lax.all_to_all(
+                jnp.stack(jnp.split(values, lax.axis_size("head"), axis=1)), "head", 0, 0
+            ),
+            axis=0,
+        ),
     )
     key_rows = key_all.reshape(layout)
     value_rows = value_all.reshape(layout)

time: 208 us -> 208 us (level)
  no operation moved by 1% of the time
where the time goes in v1:
time: 208 us; the launch traced here: 207 us
  waiting for transfers between devices  125 us (60%)
  blocking collectives  21.9 us (11%)
  other arithmetic  20 us (10%)
  between operations  14.3 us (7%)
  starting transfers between devices  11.1 us (5%)
  local copies, waits for them, and re-layouts  8.68 us (4%)
  matrix products  5.8 us (3%)
    all_gather x2, waiting for transfers between devices, prefix(): everything = jax.tree.map(lambda part: lax.all_gather(part, axis), array)  116 us
    all_gather x1, blocking collectives, prefix(): everything = jax.tree.map(lambda part: lax.all_gather(part, axis), array)  21.9 us
    select_n x16, other arithmetic, lap(): return jax.tree.map(lambda a, b: jnp.where(reached, a, b), new, before)  18.8 us
    all_to_all x1, waiting for transfers between devices, local(): lax.all_to_all(jnp.stack(jnp.split(values, lax.axis_size('head'), axis=1)...  5.53 us
    unnamed x13, local copies, waits for them, and re-layouts  4.54 us
    all_to_all x1, starting transfers between devices, local(): lax.all_to_all(keys, 'head', split_axis=1, concat_axis=0, tiled=True)  4.24 us
  transfers between devices with their start and end apart: 5, of which 4 were waited for; matrix products, arithmetic and copies ran while one was open for 4% of the time, Pallas kernels for 0%

profile of v1, /device:TPU:0, one launch (start us, length us, event | category | flops | bytes accessed | tf_op | source)
XLA Modules:
  0.0 206.9 jit_solution(9501611129364948338)
XLA Ops:
  7.2 1.7 copy.117
  8.9 4.2 %all-to-all-start.2 = ((bf16[32,4,1024]{2,0,1:T(8,128)(2,1)}), bf16[32,4,1024]{2,0,1:T(8,128)(2,1)S(1)}, u32[]{:S(2)}, u32[]{:S(2)}) async-start(bf16[32,4,1024]{2,0,1:T(8,128)(2,1)} %bitcast.107), calls=%async_computation.2 | async-start | bytes 524288 | tf_op jit(solution)/shard_map/all_to_all | solution.py:62
  15.8 3.3 %all-to-all-done.2 = bf16[32,4,1024]{2,0,1:T(8,128)(2,1)S(1)} async-done(((bf16[32,4,1024]{2,0,1:T(8,128)(2,1)}), bf16[32,4,1024]{2,0,1:T(8,128)(2,1)S(1)}, u32[]{:S(2)}, u32[]{:S(2)}) %all-to-all-start.2) | async-done | bytes 262176 | tf_op jit(solution)/shard_map/all_to_all | solution.py:62
  19.2 3.4 %all-to-all-start = ((bf16[4,32,1024]{2,1,0:T(8,128)(2,1)}), bf16[4,32,1024]{2,1,0:T(8,128)(2,1)S(1)}, u32[]{:S(2)}, u32[]{:S(2)}) async-start(bf16[4,32,1024]{2,1,0:T(8,128)(2,1)} %pad_maximum_fusion), calls=%async_computation | async-start | bytes 524288 | tf_op jit(solution)/shard_map/all_to_all | solution.py:64
  23.0 5.5 %all-to-all-done = bf16[4,32,1024]{2,1,0:T(8,128)(2,1)S(1)} async-done(((bf16[4,32,1024]{2,1,0:T(8,128)(2,1)}), bf16[4,32,1024]{2,1,0:T(8,128)(2,1)S(1)}, u32[]{:S(2)}, u32[]{:S(2)}) %all-to-all-start) | async-done | bytes 262176 | tf_op jit(solution)/shard_map/all_to_all | solution.py:64
  30.4 3.4 %all-to-all-start.1 = ((bf16[32,4,1024]{2,0,1:T(8,128)(2,1)}), bf16[32,4,1024]{2,0,1:T(8,128)(2,1)S(1)}, u32[]{:S(2)}, u32[]{:S(2)}) async-start(bf16[32,4,1024]{2,0,1:T(8,128)(2,1)} %bitcast.108), calls=%async_computation.1 | async-start | bytes 524288 | tf_op jit(solution)/shard_map/all_to_all | solution.py:61
  34.2 21.9 %all-gather.2 = f32[8,1,8]{2,1,0:T(1,128)S(1)} all-gather(f32[1,1,8]{2,1,0:T(1,128)S(1)} %get-tuple-element.305), channel_id=1, replica_groups=mesh['seq'=8,'head'=4] {'seq'}, dimensions={0}, use_global_device_ids=true | all-gather | bytes 288 | tf_op jit(solution)/shard_map/all_gather | solution.py:12
  56.8 46.8 %all-gather.6.cloned.1.call-done = f32[64,128,128]{2,1,0:T(8,128)} async-done(((f32[8,128,128]{2,1,0:T(8,128)}), f32[64,128,128]{2,1,0:T(8,128)}) %all-gather.6.cloned.1.call-update) | async-done | bytes 4194320 | tf_op jit(solution)/shard_map/all_gather | solution.py:12
  103.6 9.7 %while.30 = (s32[]{:T(128)}, f32[8,128,128]{2,1,0:T(8,128)S(1)}, s32[]{:T(128)}, f32[8,8]{1,0:T(8,128)S(1)}, f32[8,8,128,128]{3,2,1,0:T(8,128)}, /*index=5*/s32[]{:T(128)}, s32[]{:T(128)}) while((s32[]{:T(128)}, f32[8,128,128]{2,1,0:T(8,128)S(1)}, s32[]{:T(128)}, f32[8,8]{1,0:T(8,128)S(1)}, f32[8,8,128,128]{3,2,1,0:T(8,128)}, ...), condition=%wide.region_2.3_spmd.clone, body=%wide.region_1.2_spmd.clone.sunk | while | flops 524292 | bytes 1573073 | solution.py:25
  104.8 1.2 fusion.51
  106.1 1.2 fusion.51
  109.7 1.2 fusion.51
  110.9 1.2 fusion.51
  112.1 1.2 fusion.51
  114.4 1.3 fusion.18
  118.3 68.8 %all-gather.8.cloned.1.call-done = f32[64,128,128]{2,1,0:T(8,128)} async-done(((f32[8,128,128]{2,1,0:T(8,128)}), f32[64,128,128]{2,1,0:T(8,128)}) %all-gather.8.cloned.1.call-update) | async-done | bytes 4194320 | tf_op jit(solution)/shard_map/all_gather | solution.py:12
  187.2 9.8 %while.31 = (s32[]{:T(128)}, f32[8,128,128]{2,1,0:T(8,128)S(1)}, s32[]{:T(128)}, f32[8,8]{1,0:T(8,128)S(1)}, f32[8,8,128,128]{3,2,1,0:T(8,128)}, /*index=5*/s32[]{:T(128)}, s32[]{:T(128)}, s32[]{:T(128)}, s32[]{:T(128)}) while((s32[]{:T(128)}, f32[8,128,128]{2,1,0:T(8,128)S(1)}, s32[]{:T(128)}, f32[8,8]{1,0:T(8,128)S(1)}, ...), condition=%wide.region_6.7_spmd.clone, body=%wide.region_5.6_spmd.clone.sunk | while | flops 524296 | bytes 1573135 | solution.py:25
  188.4 1.2 fusion.52
  189.6 1.2 fusion.52
  190.8 1.2 fusion.52
  192.1 1.2 fusion.52
  193.3 1.2 fusion.52
  194.5 1.2 fusion.52
  195.7 1.2 fusion.52
  (67 shorter events, 17.5 us)
Async XLA Ops:
  7.2 22.5 %copy-start = (bf16[32,4096]{1,0:T(8,128)(2,1)S(1)}, bf16[32,4096]{1,0:T(8,128)(2,1)}, u32[]{:S(2)}) copy-start(bf16[32,4096]{1,0:T(8,128)(2,1)} %param.9) | copy-start | bytes 786436
  7.2 26.9 %copy-start.1 = (bf16[128,1024]{1,0:T(8,128)(2,1)S(1)}, bf16[128,1024]{1,0:T(8,128)(2,1)}, u32[]{:S(2)}) copy-start(bf16[128,1024]{1,0:T(8,128)(2,1)} %param.13) | copy-start | bytes 786436
  8.9 10.2 %all-to-all-start.2 = ((bf16[32,4,1024]{2,0,1:T(8,128)(2,1)}), bf16[32,4,1024]{2,0,1:T(8,128)(2,1)S(1)}, u32[]{:S(2)}, u32[]{:S(2)}) async-start(bf16[32,4,1024]{2,0,1:T(8,128)(2,1)} %bitcast.107), calls=%async_computation.2 | async-start | bytes 524288 | tf_op jit(solution)/shard_map/all_to_all | solution.py:62
  19.2 9.4 %all-to-all-start = ((bf16[4,32,1024]{2,1,0:T(8,128)(2,1)}), bf16[4,32,1024]{2,1,0:T(8,128)(2,1)S(1)}, u32[]{:S(2)}, u32[]{:S(2)}) async-start(bf16[4,32,1024]{2,1,0:T(8,128)(2,1)} %pad_maximum_fusion), calls=%async_computation | async-start | bytes 524288 | tf_op jit(solution)/shard_map/all_to_all | solution.py:64
  22.6 81.1 %all-gather.6.cloned.1.call-start = ((), (), s32[]{:S(2)}) async-start(), calls=%async_computation.3 | async-start | bytes 4718592 | tf_op jit(solution)/shard_map/all_gather | solution.py:12
  30.4 25.7 %all-to-all-start.1 = ((bf16[32,4,1024]{2,0,1:T(8,128)(2,1)}), bf16[32,4,1024]{2,0,1:T(8,128)(2,1)S(1)}, u32[]{:S(2)}, u32[]{:S(2)}) async-start(bf16[32,4,1024]{2,0,1:T(8,128)(2,1)} %bitcast.108), calls=%async_computation.1 | async-start | bytes 524288 | tf_op jit(solution)/shard_map/all_to_all | solution.py:61
  33.9 153.3 %all-gather.8.cloned.1.call-start = ((), (), s32[]{:S(2)}) async-start(), calls=%async_computation.4 | async-start | bytes 4718592 | tf_op jit(solution)/shard_map/all_gather | solution.py:12
Sparse Core Ops, SparseCore 0:
  29.8 73.7 all-gather.5
  115.8 71.3 all-gather.7
